TPU v7x, 256 devices: a whole 4x4x8 slice. The times are simulated.
256 devices in a mesh: gx: 32 (over y, x, core), gz: 8 (over z).
Axes of the slice: x: 4, y: 4, z: 8, core: 2. Of those that a mesh axis runs over, the one named last changes fastest.
Arguments:
- velocity: float32 [64, 3, 128, 64, 256], P(None, None, 'gx', 'gz'), may hold values from -40 to 40
- scaled_modes: float32 [64, 128, 64, 256], P(None, 'gx', 'gz'), may hold values from -70 to 70
Outputs:
- orthonormal: float32 [128, 128, 64, 256], P(None, 'gx', 'gz')
- triangle: float32 [128, 128], replicated
- lower_one: float32 [128, 128], replicated
All inputs are finite; a program needn't handle non-finite values.
Results may differ from a plain program's by a relative error of at most 0.0003.
Values sent between devices are 32-bit elements; how exact they have to be, the bound alone decides.
No kernel may reach another device: no remote copies, remote signals or barrier semaphores. Data moves between devices by JAX's collectives and lax.ppermute only.
A program may use at most 128 MiB of HBM per device.

v0:
```python
import jax
import jax.numpy as jnp
from jax import lax
from jax.sharding import PartitionSpec as P

precise = lax.Precision.HIGHEST


def with_halo(block, sides, width):
    for axis, dim in sides:
        count = lax.axis_size(axis)
        forward = [(i, i + 1) for i in range(count - 1)]
        forward.append((count - 1, 0))
        backward = [(target, source) for source, target in forward]
        low = lax.ppermute(
            lax.slice_in_dim(block, block.shape[dim] - width, None, axis=dim), axis, forward
        )
        high = lax.ppermute(lax.slice_in_dim(block, 0, width, axis=dim), axis, backward)
        block = jnp.concatenate([low, block, high], axis=dim)
    return block


def along_wall(field):
    inner = (field[..., 2:] - field[..., :-2]) * 0.5
    bottom = (-3.0 * field[..., 0:1] + 4.0 * field[..., 1:2] - field[..., 2:3]) * 0.5
    top_side = (3.0 * field[..., -1:] - 4.0 * field[..., -2:-1] + field[..., -3:-2]) * 0.5
    return jnp.concatenate([bottom, inner, top_side], -1)


def product(left, right):
    return lax.dot_general(left, right, (((1,), (1,)), ((), ())), precision=precise)


def shards(velocity, scaled_modes):
    snapshots, _, cells_x, cells_z, cells_y = velocity.shape
    columns_old = scaled_modes.shape[0]
    total_cells = cells_x * lax.axis_size("gx") * cells_z * lax.axis_size("gz") * cells_y
    mode_fields = scaled_modes.reshape(columns_old, -1)
    padded = with_halo(velocity, (("gx", 2), ("gz", 3)), 1)
    grad_x = (padded[:, :, 2:, 1:-1] - padded[:, :, :-2, 1:-1]) * 0.5
    grad_z = (padded[:, :, 1:-1, 2:] - padded[:, :, 1:-1, :-2]) * 0.5
    grad_y = along_wall(velocity)
    diagonal_part = (
        grad_x[:, 0] * grad_x[:, 0] + grad_z[:, 1] * grad_z[:, 1] + grad_y[:, 2] * grad_y[:, 2]
    )
    cross_part = (
        grad_z[:, 0] * grad_x[:, 1] + grad_y[:, 0] * grad_x[:, 2] + grad_y[:, 1] * grad_z[:, 2]
    )
    new_fields = (-0.5 * diagonal_part - cross_part).reshape(snapshots, -1)
    stacked = jnp.concatenate([mode_fields, new_fields], 0)
    gram_sum = lax.psum(product(stacked, stacked), ("gx", "gz"))
    lower_one = jnp.linalg.cholesky(gram_sum / total_cells)
    first_pass = lax.linalg.triangular_solve(lower_one, stacked, left_side=True, lower=True)
    second_sum = lax.psum(product(first_pass, first_pass), ("gx", "gz"))
    lower_two = jnp.linalg.cholesky(second_sum / total_cells)
    basis = lax.linalg.triangular_solve(lower_two, first_pass, left_side=True, lower=True)
    triangle = jnp.dot(lower_two.T, lower_one.T, precision=precise)
    return (basis.reshape(stacked.shape[0], cells_x, cells_z, cells_y), triangle, lower_one)


def solution(mesh):
    in_specs = (P(None, None, "gx", "gz", None), P(None, "gx", "gz", None))
    out_specs = (P(None, "gx", "gz", None), P(), P())
    return jax.shard_map(shards, mesh=mesh, in_specs=in_specs, out_specs=out_specs, check_vma=False)
```

profile of v0, /device:TPU:1, one launch (start us, length us, event | category | flops | bytes accessed | tf_op | source)
XLA Modules:
  0.0 683.3 jit_solution(10335882637036311948)
XLA Ops:
  7.2 6.4 copy.45
  13.7 2.7 copy-done.1
  18.3 2.6 collective-permute-start.1
  21.5 7.7 %fusion.32 = (f32[64,3,4,8,1]{4,3,2,1,0:T(8,128)}, f32[64,3,4,8,1]{4,3,2,1,0:T(8,128)}, f32[64,3,4,8,1]{4,3,2,1,0:T(8,128)}, f32[64,3,4,8,1]{4,3,2,1,0:T(8,128)}...) fusion(f32[64,3,4,8,256]{4,3,2,1,0:T(8,128)S(1)} %copy-done), kind=kLoop, calls=%fused_computation.59 | loop fusion | bytes 294912 | tf_op jit(solution)/shard_map/slice | solution.py:25
  29.2 2.7 copy.66
  31.9 2.7 copy.67
  34.6 2.7 copy.68
  37.2 2.7 copy.69
  39.9 2.7 copy.70
  44.0 2.3 copy.57
  46.3 2.5 copy.58
  48.8 2.5 copy.72
  51.3 9.2 %fusion = f32[64,3,4,8,254]{4,0,3,2,1:T(8,128)} fusion(f32[64,3,4,8,256]{4,0,3,2,1:T(8,128)} %copy-done.1), kind=kLoop, calls=%fused_computation.1 | loop fusion | flops 3121152 | bytes 18726912 | tf_op jit(solution)/shard_map/mul | solution.py:24
  60.5 7.3 %pad_maximum_fusion.4 = f32[64,3,4,8,256]{4,0,3,2,1:T(8,128)S(1)} fusion(f32[64,3,4,8,1]{4,0,3,2,1:T(8,128)} %copy.58, f32[64,3,4,8,254]{4,0,3,2,1:T(8,128)} %fusion, f32[64,3,4,8,1]{4,0,3,2,1:T(8,128)} %copy.57), kind=kLoop, calls=%fused_computation.10 | loop fusion | flops 3145728 | bytes 12582912 | tf_op jit(solution)/shard_map/concatenate | solution.py:27
  69.3 4.1 constant_dynamic-update-slice_fusion.1
  75.3 5.2 collective-permute-start.2
  82.0 12.6 %fusion.4 = f32[64,3,4,8,256]{4,0,3,2,1:T(8,128)S(1)} fusion(f32[64,3,4,8,256]{4,0,3,2,1:T(8,128)S(1)} %bitcast.38, f32[64,3,1,8,256]{4,0,3,2,1:T(8,128)} %collective-permute-done.1, f32[64,3,1,8,256]{4,0,3,2,1:T(8,128)} %collective-permute-done), kind=kLoop, calls=%fused_computation.8 | loop fusion | flops 6291456 | bytes 15728640 | tf_op jit(solution)/shard_map/mul | solution.py:40
  94.5 7.4 %collective-permute-done.2 = f32[64,3,6,1,256]{4,0,3,2,1:T(8,128)S(1)} collective-permute-done((f32[64,3,6,1,256]{4,0,3,2,1:T(8,128)S(1)}, f32[64,3,6,1,256]{4,0,3,2,1:T(8,128)S(1)}, u32[]{:S(2)}, u32[]{:S(2)}) %collective-permute-start.2) | collective-permute-done | bytes 1179680 | tf_op jit(solution)/shard_map/ppermute | solution.py:18
  102.0 3.1 collective-permute-done.3
  105.1 2.1 fusion.2
  109.3 2.6 copy.59
  115.0 7.6 %fusion.34 = f32[128,128]{0,1:T(8,128)} fusion(f32[128,8192]{1,0:T(8,128)} %constant_dynamic-update-slice_fusion.3), kind=kOutput, calls=%fused_computation.61 | convolution fusion | flops 1610612736 | bytes 4259840 | tf_op jit(solution)/shard_map/dot_general | solution.py:31
  122.7 243.7 %all-reduce.3.cloned.1.call-done = f32[128,128]{0,1:T(8,128)} async-done(((f32[128,128]{0,1:T(8,128)}), f32[128,128]{0,1:T(8,128)}) %all-reduce.3.cloned.1.call-update) | async-done | bytes 65552 | tf_op jit(solution)/shard_map/psum | solution.py:51
  368.2 11.7 %cholesky.44 = f32[128,128]{1,0:T(8,128)S(1)} custom-call(f32[128,128]{1,0:T(8,128)S(1)} %fusion.16), custom_call_target="Cholesky" | custom-call | tf_op jit(solution)/shard_map/jit(cholesky)/cholesky | solution.py:52
  381.3 9.8 %custom-call.6 = f32[1,128,128]{1,2,0:T(8,128)S(1)} custom-call(f32[1,128,128]{2,1,0:T(8,128)S(1)} %get-tuple-element.5), custom_call_target="InvertDiagBlocksLowerTriangular" | custom-call | tf_op jit(solution)/shard_map/triangular_solve/custom-call.0 | solution.py:53
  391.1 5.7 fusion.14
  398.8 4.0 fusion.35
  402.8 237.9 %all-reduce.5.cloned.1.call-done = f32[128,128]{0,1:T(8,128)} async-done(((f32[128,128]{0,1:T(8,128)}), f32[128,128]{0,1:T(8,128)}) %all-reduce.5.cloned.1.call-update) | async-done | bytes 65552 | tf_op jit(solution)/shard_map/psum | solution.py:54
  642.5 11.7 %cholesky.55 = f32[128,128]{1,0:T(8,128)S(1)} custom-call(f32[128,128]{1,0:T(8,128)S(1)} %fusion.13), custom_call_target="Cholesky" | custom-call | tf_op jit(solution)/shard_map/jit(cholesky)/cholesky | solution.py:55
  657.1 9.8 %custom-call.7 = f32[1,128,128]{1,2,0:T(8,128)S(1)} custom-call(f32[1,128,128]{2,1,0:T(8,128)S(1)} %select_bitcast_fusion), custom_call_target="InvertDiagBlocksLowerTriangular" | custom-call | tf_op jit(solution)/shard_map/triangular_solve/custom-call.0 | solution.py:56
  667.0 5.7 fusion.11
  672.7 3.3 copy.73
  (53 shorter events, 24.2 us)
Async XLA Ops:
  7.2 359.2 %all-reduce.3.cloned.1.call-start = ((), (), s32[]{:S(2)}) async-start(), calls=%async_computation | async-start | bytes 131072 | tf_op jit(solution)/shard_map/psum | solution.py:51
  13.6 2.7 copy-start.1
  16.3 5.2 copy-start
  18.3 49.5 %collective-permute-start.1 = (f32[64,3,1,8,256]{4,0,3,2,1:T(8,128)}, f32[64,3,1,8,256]{4,0,3,2,1:T(8,128)}, u32[]{:S(2)}, u32[]{:S(2)}) collective-permute-start(f32[64,3,1,8,256]{4,0,3,2,1:T(8,128)} %get-tuple-element.16), channel_id=1, source_target_pairs={{0,8},{8,16},{16,24},{24,32},{32,40},{40,48},{48,56},{56,64},{64,7... | collective-permute-start | bytes 4718600 | tf_op jit(solution)/shard_map/ppermute | solution.py:15
  20.9 52.5 %collective-permute-start = (f32[64,3,1,8,256]{4,0,3,2,1:T(8,128)}, f32[64,3,1,8,256]{4,0,3,2,1:T(8,128)}, u32[]{:S(2)}, u32[]{:S(2)}) collective-permute-start(f32[64,3,1,8,256]{4,0,3,2,1:T(8,128)} %get-tuple-element.15), channel_id=1, source_target_pairs={{8,0},{16,8},{24,16},{32,24},{40,32},{48,40},{56,48},{64,56},{72,6... | collective-permute-start | bytes 4718600 | tf_op jit(solution)/shard_map/ppermute | solution.py:18
  44.0 4.8 copy-start.4
  51.3 18.0 %slice-start = ((s8[6291456]{0:T(1024)(128)(4,1)}), s8[4194304]{0:T(1024)(128)(4,1)S(1)}, s32[]{:S(2)}) async-start(s8[6291456]{0:T(1024)(128)(4,1)} %bitcast.35), calls=%async_computation.2 | async-start | bytes 8388608
  60.5 8.8 %slice-start.1 = ((s8[6291456]{0:T(1024)(128)(4,1)}), s8[2097152]{0:T(1024)(128)(4,1)S(1)}, s32[]{:S(2)}) async-start(s8[6291456]{0:T(1024)(128)(4,1)} %bitcast.35), calls=%async_computation.3 | async-start | bytes 4194304
  73.4 7.1 %copy-start.3 = (f32[8,8,32,256]{3,1,2,0:T(8,128)S(1)}, f32[8,8,32,256]{3,1,2,0:T(8,128)}, u32[]{:S(2)}) copy-start(f32[8,8,32,256]{3,1,2,0:T(8,128)} %copy.72) | copy-start | bytes 6291460
  73.4 8.6 %slice-start.2 = ((s8[6291456]{0:T(1024)(128)(4,1)}), s8[4194304]{0:T(1024)(128)(4,1)S(1)}, s32[]{:S(2)}) async-start(s8[6291456]{0:T(1024)(128)(4,1)} %bitcast.37), calls=%async_computation.4 | async-start | bytes 8388608
  75.1 6.9 %slice-start.3 = ((s8[6291456]{0:T(1024)(128)(4,1)}), s8[2097152]{0:T(1024)(128)(4,1)S(1)}, s32[]{:S(2)}) async-start(s8[6291456]{0:T(1024)(128)(4,1)} %bitcast.37), calls=%async_computation.5 | async-start | bytes 4194304
  75.3 26.6 %collective-permute-start.2 = (f32[64,3,6,1,256]{4,0,3,2,1:T(8,128)S(1)}, f32[64,3,6,1,256]{4,0,3,2,1:T(8,128)S(1)}, u32[]{:S(2)}, u32[]{:S(2)}) collective-permute-start(f32[64,3,6,1,256]{4,0,3,2,1:T(8,128)S(1)} %get-tuple-element.7), channel_id=1, source_target_pairs={{1,0},{2,1},{3,2},{4,3},{5,4},{6,5},{7,6},{0,7},{9,8},{10,9},{11,1... | collective-permute-start | bytes 3538952 | tf_op jit(solution)/shard_map/ppermute | solution.py:18
  80.5 24.6 %collective-permute-start.3 = (f32[64,3,6,1,256]{4,0,3,2,1:T(8,128)S(1)}, f32[64,3,6,1,256]{4,0,3,2,1:T(8,128)S(1)}, u32[]{:S(2)}, u32[]{:S(2)}) collective-permute-start(f32[64,3,6,1,256]{4,0,3,2,1:T(8,128)S(1)} %get-tuple-element.8), channel_id=1, source_target_pairs={{0,1},{1,2},{2,3},{3,4},{4,5},{5,6},{6,7},{7,0},{8,9},{9,10},{10,1... | collective-permute-start | bytes 3538952 | tf_op jit(solution)/shard_map/ppermute | solution.py:15
  122.7 518.0 %all-reduce.5.cloned.1.call-start = ((), (), s32[]{:S(2)}) async-start(), calls=%async_computation.1 | async-start | bytes 131072 | tf_op jit(solution)/shard_map/psum | solution.py:54
  381.3 274.3 %copy-start.5 = (f32[128,128]{1,0:T(8,128)}, f32[128,128]{1,0:T(8,128)S(1)}, u32[]{:S(2)}) copy-start(f32[128,128]{1,0:T(8,128)S(1)} %get-tuple-element.6) | copy-start | bytes 196612
  396.7 2.0 copy-start.2
Sparse Core Ops, SparseCore 0:
  122.8 243.5 all-reduce.2
  402.9 237.7 all-reduce.4
where the time goes:
time: 692 us; the launch traced here: 683 us
  waiting for transfers between devices  492 us (71%)
  other arithmetic  82.3 us (12%)
  local copies, waits for them, and re-layouts  61 us (9%)
  matrix products  24.5 us (4%)
  between operations  14.8 us (2%)
  starting transfers between devices  8.45 us (1%)
    psum x1, waiting for transfers between devices, shards(): gram_sum = lax.psum(product(stacked, stacked), ('gx', 'gz'))  244 us
    psum x1, waiting for transfers between devices, shards(): second_sum = lax.psum(product(first_pass, first_pass), ('gx', 'gz'))  238 us
    unnamed x32, local copies, waits for them, and re-layouts  38.8 us
  transfers between devices with their start and end apart: 6, of which 4 were waited for; matrix products, arithmetic and copies ran while one was open for 10% of the time, Pallas kernels for 0%

commit v1 on v0

--- a/solution.py
+++ b/solution.py
@@ -1,9 +1,17 @@
+import functools
 import jax
 import jax.numpy as jnp
 from jax import lax
 from jax.sharding import PartitionSpec as P
 
 precise = lax.Precision.HIGHEST
+
+
+def _compute_pieces_all(work_x, axis_key, peer_axis):
+    return lax.psum(lax.psum(work_x, axis_name=axis_key), peer_axis)
+
+
+convert_roads_on_mesh = functools.partial(_compute_pieces_all, axis_key="gx", peer_axis="gz")
 
 
 def with_halo(block, sides, width):
@@ -51,7 +59,7 @@
     gram_sum = lax.psum(product(stacked, stacked), ("gx", "gz"))
     lower_one = jnp.linalg.cholesky(gram_sum / total_cells)
     first_pass = lax.linalg.triangular_solve(lower_one, stacked, left_side=True, lower=True)
-    second_sum = lax.psum(product(first_pass, first_pass), ("gx", "gz"))
+    second_sum = convert_roads_on_mesh(product(first_pass, first_pass))
     lower_two = jnp.linalg.cholesky(second_sum / total_cells)
     basis = lax.linalg.triangular_solve(lower_two, first_pass, left_side=True, lower=True)
     triangle = jnp.dot(lower_two.T, lower_one.T, precision=precise)

time: 692 us -> 629 us (0.909)
  the two profiles are of different devices: /device:TPU:1 before, /device:TPU:2 now
where the time goes in v1:
time: 629 us; the launch traced here: 621 us
  waiting for transfers between devices  440 us (70%)
  other arithmetic  72.6 us (12%)
  local copies, waits for them, and re-layouts  61.1 us (10%)
  matrix products  24.1 us (4%)
  between operations  14.2 us (2%)
  starting transfers between devices  8.38 us (1%)
    psum x1, waiting for transfers between devices, shards(): gram_sum = lax.psum(product(stacked, stacked), ('gx', 'gz'))  238 us
    psum x2, waiting for transfers between devices, _compute_pieces_all(): return lax.psum(lax.psum(work_x, axis_name=axis_key), peer_axis)  178 us
    unnamed x32, local copies, waits for them, and re-layouts  38.9 us
    ppermute x2, waiting for transfers between devices, with_halo(): lax.ppermute(lax.slice_in_dim(block, 0, width, axis=dim), axis, backward)  20.9 us
  transfers between devices with their start and end apart: 7, of which 5 were waited for; matrix products, arithmetic and copies ran while one was open for 9% of the time, Pallas kernels for 0%

profile of v1, /device:TPU:2, one launch (start us, length us, event | category | flops | bytes accessed | tf_op | source)
XLA Modules:
  0.0 620.6 jit_solution(11998191761671767725)
XLA Ops:
  7.2 6.4 %copy.45 = f32[64,3,4,8,256]{4,0,3,2,1:T(8,128)S(1)} copy(f32[64,3,4,8,256]{4,3,2,1,0:T(8,128)} %param.5) | data formatting | bytes 12582912 | tf_op args[0]
  13.7 2.7 copy-done.1
  20.2 7.7 %fusion.32 = (f32[64,3,4,8,1]{4,3,2,1,0:T(8,128)}, f32[64,3,4,8,1]{4,3,2,1,0:T(8,128)}, f32[64,3,4,8,1]{4,3,2,1,0:T(8,128)}, f32[64,3,4,8,1]{4,3,2,1,0:T(8,128)}...) fusion(f32[64,3,4,8,256]{4,3,2,1,0:T(8,128)S(1)} %copy-done), kind=kLoop, calls=%fused_computation.59 | loop fusion | bytes 294912 | tf_op jit(solution)/shard_map/slice | solution.py:33
  27.9 2.7 copy.66
  30.6 2.7 copy.67
  33.2 2.7 copy.68
  35.9 2.7 copy.69
  38.6 2.7 copy.70
  42.7 2.3 copy.57
  45.0 2.4 copy.58
  47.4 2.5 copy.72
  49.9 9.2 %fusion = f32[64,3,4,8,254]{4,0,3,2,1:T(8,128)} fusion(f32[64,3,4,8,256]{4,0,3,2,1:T(8,128)} %copy-done.1), kind=kLoop, calls=%fused_computation.1 | loop fusion | flops 3121152 | bytes 18726912 | tf_op jit(solution)/shard_map/mul | solution.py:32
  59.1 7.3 %pad_maximum_fusion.4 = f32[64,3,4,8,256]{4,0,3,2,1:T(8,128)S(1)} fusion(f32[64,3,4,8,1]{4,0,3,2,1:T(8,128)} %copy.58, f32[64,3,4,8,254]{4,0,3,2,1:T(8,128)} %fusion, f32[64,3,4,8,1]{4,0,3,2,1:T(8,128)} %copy.57), kind=kLoop, calls=%fused_computation.10 | loop fusion | flops 3145728 | bytes 12582912 | tf_op jit(solution)/shard_map/concatenate | solution.py:35
  67.9 4.1 constant_dynamic-update-slice_fusion.1
  73.9 5.9 collective-permute-start.2
  81.4 2.8 fusion.4
  84.2 20.9 %collective-permute-done.2 = f32[64,3,6,1,256]{4,0,3,2,1:T(8,128)S(1)} collective-permute-done((f32[64,3,6,1,256]{4,0,3,2,1:T(8,128)S(1)}, f32[64,3,6,1,256]{4,0,3,2,1:T(8,128)S(1)}, u32[]{:S(2)}, u32[]{:S(2)}) %collective-permute-start.2) | collective-permute-done | bytes 1179680 | tf_op jit(solution)/shard_map/ppermute | solution.py:26
  105.1 3.4 collective-permute-done.3
  108.5 2.1 fusion.2
  112.7 2.6 copy.59
  118.4 7.6 %fusion.34 = f32[128,128]{0,1:T(8,128)} fusion(f32[128,8192]{1,0:T(8,128)} %constant_dynamic-update-slice_fusion.3), kind=kOutput, calls=%fused_computation.61 | convolution fusion | flops 1610612736 | bytes 4259840 | tf_op jit(solution)/shard_map/dot_general | solution.py:39
  126.5 237.7 %all-reduce.4.cloned.1.call-done = f32[128,128]{0,1:T(8,128)} async-done(((f32[128,128]{0,1:T(8,128)}), f32[128,128]{0,1:T(8,128)}) %all-reduce.4.cloned.1.call-update) | async-done | bytes 65552 | tf_op jit(solution)/shard_map/psum | solution.py:59
  366.1 11.7 %cholesky.44 = f32[128,128]{1,0:T(8,128)S(1)} custom-call(f32[128,128]{1,0:T(8,128)S(1)} %fusion.16), custom_call_target="Cholesky" | custom-call | tf_op jit(solution)/shard_map/jit(cholesky)/cholesky | solution.py:60
  379.1 9.8 %custom-call.6 = f32[1,128,128]{1,2,0:T(8,128)S(1)} custom-call(f32[1,128,128]{2,1,0:T(8,128)S(1)} %get-tuple-element.5), custom_call_target="InvertDiagBlocksLowerTriangular" | custom-call | tf_op jit(solution)/shard_map/triangular_solve/custom-call.0 | solution.py:61
  388.9 5.4 fusion.14
  396.4 4.0 fusion.35
  400.7 103.7 %all-reduce.6.cloned.1.call-done = f32[128,128]{0,1:T(8,128)} async-done(((f32[128,128]{0,1:T(8,128)}), f32[128,128]{0,1:T(8,128)}) %all-reduce.6.cloned.1.call-update) | async-done | bytes 65552 | tf_op jit(solution)/shard_map/psum | solution.py:11
  504.5 74.4 %all-reduce.8.cloned.1.call-done = f32[128,128]{0,1:T(8,128)} async-done(((f32[128,128]{0,1:T(8,128)}), f32[128,128]{0,1:T(8,128)}) %all-reduce.8.cloned.1.call-update) | async-done | bytes 65552 | tf_op jit(solution)/shard_map/psum | solution.py:11
  580.7 11.7 %cholesky.55 = f32[128,128]{1,0:T(8,128)S(1)} custom-call(f32[128,128]{1,0:T(8,128)S(1)} %fusion.13), custom_call_target="Cholesky" | custom-call | tf_op jit(solution)/shard_map/jit(cholesky)/cholesky | solution.py:63
  595.3 9.8 %custom-call.7 = f32[1,128,128]{1,2,0:T(8,128)S(1)} custom-call(f32[1,128,128]{2,1,0:T(8,128)S(1)} %select_bitcast_fusion), custom_call_target="InvertDiagBlocksLowerTriangular" | custom-call | tf_op jit(solution)/shard_map/triangular_solve/custom-call.0 | solution.py:64
  605.1 5.4 fusion.11
  610.6 3.3 copy.73
  (56 shorter events, 26.1 us)
Async XLA Ops:
  7.2 357.1 %all-reduce.4.cloned.1.call-start = ((), (), s32[]{:S(2)}) async-start(), calls=%async_computation | async-start | bytes 131072 | tf_op jit(solution)/shard_map/psum | solution.py:59
  13.6 2.7 copy-start.1
  16.3 3.9 copy-start
  18.3 48.1 %collective-permute-start.1 = (f32[64,3,1,8,256]{4,0,3,2,1:T(8,128)}, f32[64,3,1,8,256]{4,0,3,2,1:T(8,128)}, u32[]{:S(2)}, u32[]{:S(2)}) collective-permute-start(f32[64,3,1,8,256]{4,0,3,2,1:T(8,128)} %get-tuple-element.16), channel_id=1, source_target_pairs={{0,8},{8,16},{16,24},{24,32},{32,40},{40,48},{48,56},{56,64},{64,7... | collective-permute-start | bytes 4718600 | tf_op jit(solution)/shard_map/ppermute | solution.py:23
  18.3 53.7 %collective-permute-start = (f32[64,3,1,8,256]{4,0,3,2,1:T(8,128)}, f32[64,3,1,8,256]{4,0,3,2,1:T(8,128)}, u32[]{:S(2)}, u32[]{:S(2)}) collective-permute-start(f32[64,3,1,8,256]{4,0,3,2,1:T(8,128)} %get-tuple-element.15), channel_id=1, source_target_pairs={{8,0},{16,8},{24,16},{32,24},{40,32},{48,40},{56,48},{64,56},{72,6... | collective-permute-start | bytes 4718600 | tf_op jit(solution)/shard_map/ppermute | solution.py:26
  42.7 4.7 copy-start.4
  49.9 18.0 %slice-start = ((s8[6291456]{0:T(1024)(128)(4,1)}), s8[4194304]{0:T(1024)(128)(4,1)S(1)}, s32[]{:S(2)}) async-start(s8[6291456]{0:T(1024)(128)(4,1)} %bitcast.35), calls=%async_computation.3 | async-start | bytes 8388608
  59.1 8.8 %slice-start.1 = ((s8[6291456]{0:T(1024)(128)(4,1)}), s8[2097152]{0:T(1024)(128)(4,1)S(1)}, s32[]{:S(2)}) async-start(s8[6291456]{0:T(1024)(128)(4,1)} %bitcast.35), calls=%async_computation.4 | async-start | bytes 4194304
  72.0 7.9 %copy-start.3 = (f32[8,8,32,256]{3,1,2,0:T(8,128)S(1)}, f32[8,8,32,256]{3,1,2,0:T(8,128)}, u32[]{:S(2)}) copy-start(f32[8,8,32,256]{3,1,2,0:T(8,128)} %copy.72) | copy-start | bytes 6291460
  72.0 9.3 %slice-start.2 = ((s8[6291456]{0:T(1024)(128)(4,1)}), s8[4194304]{0:T(1024)(128)(4,1)S(1)}, s32[]{:S(2)}) async-start(s8[6291456]{0:T(1024)(128)(4,1)} %bitcast.37), calls=%async_computation.5 | async-start | bytes 8388608
  73.7 7.6 %slice-start.3 = ((s8[6291456]{0:T(1024)(128)(4,1)}), s8[2097152]{0:T(1024)(128)(4,1)S(1)}, s32[]{:S(2)}) async-start(s8[6291456]{0:T(1024)(128)(4,1)} %bitcast.37), calls=%async_computation.6 | async-start | bytes 4194304
  73.9 31.2 %collective-permute-start.2 = (f32[64,3,6,1,256]{4,0,3,2,1:T(8,128)S(1)}, f32[64,3,6,1,256]{4,0,3,2,1:T(8,128)S(1)}, u32[]{:S(2)}, u32[]{:S(2)}) collective-permute-start(f32[64,3,6,1,256]{4,0,3,2,1:T(8,128)S(1)} %get-tuple-element.7), channel_id=1, source_target_pairs={{1,0},{2,1},{3,2},{4,3},{5,4},{6,5},{7,6},{0,7},{9,8},{10,9},{11,1... | collective-permute-start | bytes 3538952 | tf_op jit(solution)/shard_map/ppermute | solution.py:26
  79.9 28.6 %collective-permute-start.3 = (f32[64,3,6,1,256]{4,0,3,2,1:T(8,128)S(1)}, f32[64,3,6,1,256]{4,0,3,2,1:T(8,128)S(1)}, u32[]{:S(2)}, u32[]{:S(2)}) collective-permute-start(f32[64,3,6,1,256]{4,0,3,2,1:T(8,128)S(1)} %get-tuple-element.8), channel_id=1, source_target_pairs={{0,1},{1,2},{2,3},{3,4},{4,5},{5,6},{6,7},{7,0},{8,9},{9,10},{10,1... | collective-permute-start | bytes 3538952 | tf_op jit(solution)/shard_map/ppermute | solution.py:23
  126.1 378.4 %all-reduce.6.cloned.1.call-start = ((), (), s32[]{:S(2)}) async-start(), calls=%async_computation.1 | async-start | bytes 131072 | tf_op jit(solution)/shard_map/psum | solution.py:11
  379.1 214.7 %copy-start.5 = (f32[128,128]{1,0:T(8,128)}, f32[128,128]{1,0:T(8,128)S(1)}, u32[]{:S(2)}) copy-start(f32[128,128]{1,0:T(8,128)S(1)} %get-tuple-element.6) | copy-start | bytes 196612
  394.4 2.0 copy-start.2
  400.5 178.4 %all-reduce.8.cloned.1.call-start = ((), (), s32[]{:S(2)}) async-start(), calls=%async_computation.2 | async-start | bytes 131072 | tf_op jit(solution)/shard_map/psum | solution.py:11
Sparse Core Ops, SparseCore 0:
  126.2 238.0 all-reduce.3
  400.6 103.7 all-reduce.5
  506.7 72.1 all-reduce.7
